TPU v7x, 128 devices: a whole 4x4x4 slice. The times are simulated.
128 devices in a mesh: expert: 8 (over y, z_lo), fsdp: 16 (over x, z_hi, core).
Axes of the slice: x: 4, y: 4, z: 4 (z_hi: 2, z_lo: 2; z = z_hi * 2 + z_lo), core: 2. Of those that a mesh axis runs over, the one named last changes fastest.
Arguments:
- tokens: bfloat16 [18432, 2048], P(('expert', 'fsdp')), may hold values from -6 to 6
- expert_ids: int32 [18432, 6], P(('expert', 'fsdp')), may hold values from 0 to 15, as said below
- combine: float32 [18432, 6], P(('expert', 'fsdp')), may hold values from 0.05 to 1
- gate_weight: bfloat16 [16, 1408, 2048], P('expert', 'fsdp'), may hold values from -0.125 to 0.125
- up_weight: bfloat16 [16, 1408, 2048], P('expert', 'fsdp'), may hold values from -0.125 to 0.125
- down_weight: bfloat16 [16, 1408, 2048], P('expert', 'fsdp'), may hold values from -0.15625 to 0.15625
Outputs:
- mixed: bfloat16 [18432, 2048], P(('expert', 'fsdp'))
Inputs may be any that keep to these rules, and one draw needn't show every extreme that they name: `expert_ids`: each row names 6 different experts. Within the 144 rows of each device no expert is named more than 72 times, and one and the same expert is named exactly 72 times by the rows of every device.
All inputs are finite; a program needn't handle non-finite values.
Results may differ from a plain program's by a relative error of at most 0.0058.
Values may be sent and summed in bfloat16 or wider, within the bound.
A program may use at most 128 MiB of HBM per device.

v0:
```python
import jax
import jax.numpy as jnp
from jax import lax
from jax.sharding import Mesh
from jax.sharding import PartitionSpec as P

CAP = 72


def gather_expert(piece, core):
    mine = lax.dynamic_index_in_dim(piece, core, 0, keepdims=False)
    other = lax.dynamic_index_in_dim(piece, 1 - core, 0, keepdims=False)
    got = lax.ppermute(other, "core", [(0, 1), (1, 0)])
    pair = jnp.stack([mine, got])
    return lax.all_gather(pair, "chip", axis=0, tiled=True).reshape(-1, piece.shape[-1])


def per_device(tokens, expert_ids, combine, gate_weight, up_weight, down_weight):
    core = lax.axis_index("core")
    per_group = gate_weight.shape[0]
    groups = lax.axis_size("expert")
    n_expert = per_group * groups
    tok_rows, top_k = expert_ids.shape
    model_width = tokens.shape[1]
    gate_full = gather_expert(gate_weight, core)
    up_full = gather_expert(up_weight, core)
    down_full = gather_expert(down_weight, core)
    flat_ids = expert_ids.reshape(-1)
    onehot = (flat_ids[:, None] == jnp.arange(n_expert, dtype=jnp.int32)[None, :]).astype(jnp.int32)
    earlier = jnp.cumsum(onehot, axis=0) - onehot
    rank_within = jnp.sum(earlier * onehot, axis=1)
    slot_index = flat_ids * CAP + rank_within
    source = jnp.arange(tok_rows * top_k, dtype=jnp.int32) // top_k
    outgoing = (
        jnp.zeros((n_expert * CAP, model_width), jnp.bfloat16).at[slot_index].set(tokens[source])
    )
    outgoing = outgoing.reshape(n_expert, CAP, model_width)
    arrived = lax.all_to_all(outgoing, ("expert", "core"), 0, 0, tiled=True)
    rows = arrived.reshape(n_expert * CAP, model_width)
    gate_pre = jnp.dot(rows, gate_full.T, preferred_element_type=jnp.float32)
    up_pre = jnp.dot(rows, up_full.T, preferred_element_type=jnp.float32)
    hidden = (jax.nn.silu(gate_pre) * up_pre).astype(jnp.bfloat16)
    produced = jnp.dot(hidden, down_full, preferred_element_type=jnp.float32).astype(jnp.bfloat16)
    produced = produced.reshape(n_expert, CAP, model_width)
    returned = lax.all_to_all(produced, ("expert", "core"), 0, 0, tiled=True)
    back_rows = returned.reshape(n_expert * CAP, model_width)[slot_index]
    weighted = (
        back_rows.astype(jnp.float32).reshape(tok_rows, top_k, model_width) * combine[:, :, None]
    )
    return jnp.sum(weighted, axis=1).astype(jnp.bfloat16)


def solution(mesh):
    groups = mesh.shape["expert"]
    chips = mesh.shape["fsdp"] // 2
    inner = Mesh(mesh.devices.reshape(groups, chips, 2), ("expert", "chip", "core"))
    rows = P(("expert", "chip", "core"), None)
    weights = P("expert", ("chip", "core"), None)
    return jax.shard_map(
        per_device,
        mesh=inner,
        in_specs=(rows, rows, rows, weights, weights, weights),
        out_specs=rows,
        check_vma=False,
    )
```

profile of v0, /device:TPU:49, one launch (start us, length us, event | category | flops | bytes accessed | tf_op | source)
XLA Modules:
  0.0 445.9 jit_solution(6090683395632843541)
XLA Ops:
  6.5 1.3 constant_dynamic-slice_fusion.2
  7.8 0.8 collective-permute-start
  8.6 1.3 collective-permute-done
  9.9 0.9 pad_maximum_fusion
  10.9 1.2 constant_dynamic-slice_fusion.1
  12.1 0.5 collective-permute-start.1
  12.5 1.3 collective-permute-done.1
  13.8 0.9 pad_maximum_fusion.1
  14.8 0.1 constant_dynamic-slice_fusion
  14.9 0.5 collective-permute-start.2
  15.3 1.3 collective-permute-done.2
  16.6 0.9 pad_maximum_fusion.2
  17.6 0.1 copy.14
  17.7 0.1 eq.22
  17.9 2.0 reduce-window.6
  19.9 0.3 slice_reduce_fusion
  20.2 0.1 copy.13
  20.3 0.1 mul.36
  20.5 0.1 bitcast_bitcast_fusion
  20.7 23.1 %scatter_custom_fusion = bf16[1152,2048]{1,0:T(8,128)(2,1)} fusion(s32[864]{0:T(1024)S(1)} %fusion.6, bf16[144,2048]{1,0:T(8,128)(2,1)S(1)} %copy-done, s32[1024]{0:T(1024)S(1)} %pad_clamp_fusion.1, bf16[]{:T(256)} %constant.40.clone.1), kind=kCustom, calls=%fused_computation.7 | custom fusion | bytes 4718594 | tf_op jit(solution)/shard_map/scatter | solution.py:35
  43.8 70.3 %all_to_all.10 = bf16[16,72,2048]{2,1,0:T(8,128)(2,1)} all-to-all(bf16[16,72,2048]{2,1,0:T(8,128)(2,1)} %bitcast.43), channel_id=1, replica_groups=mesh['expert'=8,'chip'=8,'core'=2] {'expert','core'}, dimensions={0} | all-to-all | bytes 9437184 | tf_op jit(solution)/shard_map/all_to_all | solution.py:38
  114.1 32.5 %all-gather.4.cloned.1.call-done = bf16[16,88,2048]{2,1,0:T(8,128)(2,1)} async-done(((bf16[2,88,2048]{2,1,0:T(8,128)(2,1)}), bf16[16,88,2048]{2,1,0:T(8,128)(2,1)}) %all-gather.4.cloned.1.call-update) | async-done | bytes 5767184 | tf_op jit(solution)/shard_map/all_gather | solution.py:15
  146.6 12.8 %fusion.8 = f32[1152,1408]{1,0:T(8,128)} fusion(bf16[1152,2048]{1,0:T(8,128)(2,1)} %bitcast.44, bf16[1408,2048]{1,0:T(8,128)(2,1)} %bitcast.51), kind=kOutput, calls=%fused_computation.40 | convolution fusion | flops 6643777536 | bytes 16973824 | tf_op jit(solution)/shard_map/dot_general | solution.py:40
  159.4 72.2 %all-gather.6.cloned.1.call-done = bf16[16,88,2048]{2,1,0:T(8,128)(2,1)} async-done(((bf16[2,88,2048]{2,1,0:T(8,128)(2,1)}), bf16[16,88,2048]{2,1,0:T(8,128)(2,1)}) %all-gather.6.cloned.1.call-update) | async-done | bytes 5767184 | tf_op jit(solution)/shard_map/all_gather | solution.py:15
  231.6 84.9 %all-gather.8.cloned.1.call-done = bf16[16,88,2048]{2,1,0:T(8,128)(2,1)} async-done(((bf16[2,88,2048]{2,1,0:T(8,128)(2,1)}), bf16[16,88,2048]{2,1,0:T(8,128)(2,1)}) %all-gather.8.cloned.1.call-update) | async-done | bytes 5767184 | tf_op jit(solution)/shard_map/all_gather | solution.py:15
  316.5 22.7 %convolution_convert_fusion = bf16[1152,2048]{1,0:T(8,128)(2,1)} fusion(bf16[1408,2048]{1,0:T(8,128)(2,1)} %bitcast.53, bf16[1152,2048]{1,0:T(8,128)(2,1)} %bitcast.45, bf16[1408,2048]{1,0:T(8,128)(2,1)} %bitcast.52, f32[1152,1408]{1,0:T(8,128)} %fusion.8), kind=kOutput, calls=%fused_computation.6 | convolution fusion | flops 13299646464 | bytes 27459584 | tf_op jit(solution)/shard_map/dot_general | solution.py:43
  339.3 6.6 %all-to-all-start.1 = ((bf16[16,72,2048]{2,1,0:T(8,128)(2,1)}), bf16[16,72,2048]{2,1,0:T(8,128)(2,1)}, u32[]{:S(2)}, u32[]{:S(2)}) async-start(bf16[16,72,2048]{2,1,0:T(8,128)(2,1)} %bitcast.46), calls=%async_computation.1 | async-start | bytes 9437184 | tf_op jit(solution)/shard_map/all_to_all | solution.py:45
  345.8 0.1 copy.17
  346.0 66.4 %all-to-all-done.1 = bf16[16,72,2048]{2,1,0:T(8,128)(2,1)} async-done(((bf16[16,72,2048]{2,1,0:T(8,128)(2,1)}), bf16[16,72,2048]{2,1,0:T(8,128)(2,1)}, u32[]{:S(2)}, u32[]{:S(2)}) %all-to-all-start.1) | async-done | bytes 4718624 | tf_op jit(solution)/shard_map/all_to_all | solution.py:45
  412.3 11.7 %gather_fusion = bf16[864,2048]{1,0:T(8,128)(2,1)} fusion(bf16[1152,2048]{1,0:T(8,128)(2,1)} %bitcast.13, s32[1024]{0:T(1024)S(1)} %pad_clamp_fusion), kind=kCustom, calls=%fused_computation.1 | custom fusion | bytes 7081344 | tf_op jit(solution)/shard_map/gather | solution.py:46
  424.0 7.1 %reshape.120 = f32[144,6,2048]{2,1,0:T(8,128)} reshape(bf16[864,2048]{1,0:T(8,128)(2,1)} %gather_fusion) | data formatting | bytes 10616832 | tf_op jit(solution)/shard_map/convert_element_type | solution.py:48
  431.2 8.2 %multiply_reduce_fusion = bf16[144,2048]{1,0:T(8,128)(2,1)} fusion(f32[144,6,2048]{2,1,0:T(8,128)} %reshape.120, f32[144,6]{1,0:T(8,128)S(1)} %copy.17), kind=kLoop, calls=%fused_computation.4 | loop fusion | flops 3244032 | bytes 7671168 | tf_op jit(solution)/shard_map/reduce_sum | solution.py:50
  (23 shorter events, 0.3 us)
Async XLA Ops:
  6.5 14.1 %copy-start = (bf16[144,2048]{1,0:T(8,128)(2,1)S(1)}, bf16[144,2048]{1,0:T(8,128)(2,1)}, u32[]{:S(2)}) copy-start(bf16[144,2048]{1,0:T(8,128)(2,1)} %param.6) | copy-start | bytes 1769476
  6.5 8.3 %copy-start.1 = (bf16[2,88,2048]{2,1,0:T(8,128)(2,1)S(1)}, bf16[2,88,2048]{2,1,0:T(8,128)(2,1)}, u32[]{:S(2)}) copy-start(bf16[2,88,2048]{2,1,0:T(8,128)(2,1)} %param.11) | copy-start | bytes 2162692
  6.5 140.1 %all-gather.4.cloned.1.call-start = ((), (), s32[]{:S(2)}) async-start(), calls=%async_computation.2 | async-start | bytes 6488064 | tf_op jit(solution)/shard_map/all_gather | solution.py:15
  7.8 9.8 %copy-start.2 = (s32[144,6]{0,1:T(8,128)S(1)}, s32[144,6]{0,1:T(8,128)}, u32[]{:S(2)}) copy-start(s32[144,6]{0,1:T(8,128)} %param.7) | copy-start | bytes 10372
  7.8 2.1 collective-permute-start
  10.8 220.7 %all-gather.6.cloned.1.call-start = ((), (), s32[]{:S(2)}) async-start(), calls=%async_computation.3 | async-start | bytes 6488064 | tf_op jit(solution)/shard_map/all_gather | solution.py:15
  12.1 1.8 collective-permute-start.1
  14.8 301.8 %all-gather.8.cloned.1.call-start = ((), (), s32[]{:S(2)}) async-start(), calls=%async_computation.4 | async-start | bytes 6488064 | tf_op jit(solution)/shard_map/all_gather | solution.py:15
  14.9 1.8 collective-permute-start.2
  339.3 6.6 %copy-start.3 = (f32[144,6]{0,1:T(8,128)S(1)}, f32[144,6]{0,1:T(8,128)}, u32[]{:S(2)}) copy-start(f32[144,6]{0,1:T(8,128)} %param.8) | copy-start | bytes 10372
  339.3 73.1 %all-to-all-start.1 = ((bf16[16,72,2048]{2,1,0:T(8,128)(2,1)}), bf16[16,72,2048]{2,1,0:T(8,128)(2,1)}, u32[]{:S(2)}, u32[]{:S(2)}) async-start(bf16[16,72,2048]{2,1,0:T(8,128)(2,1)} %bitcast.46), calls=%async_computation.1 | async-start | bytes 9437184 | tf_op jit(solution)/shard_map/all_to_all | solution.py:45
Sparse Core Ops, SparseCore 0:
  11.0 135.6 all-gather.3
  148.9 82.5 all-gather.5
  233.9 82.5 all-gather.7
where the time goes:
time: 446 us
  waiting for transfers between devices  260 us (58%)
  blocking collectives  70.3 us (16%)
  local copies, waits for them, and re-layouts  45.4 us (10%)
  matrix products  35.5 us (8%)
  between operations  13.3 us (3%)
  other arithmetic  13.2 us (3%)
  starting transfers between devices  8.33 us (2%)
    all_gather x3, waiting for transfers between devices, gather_expert(): lax.all_gather(pair, 'chip', axis=0, tiled=True)  190 us
    all_to_all x1, blocking collectives, per_device(): arrived = lax.all_to_all(outgoing, ('expert', 'core'), 0, 0, tiled=True)  70.3 us
    all_to_all x1, waiting for transfers between devices, per_device(): returned = lax.all_to_all(produced, ('expert', 'core'), 0, 0, tiled=True)  66.4 us
    scatter x1, local copies, waits for them, and re-layouts, per_device(): jnp.zeros((n_expert * CAP, model_width), jnp.bfloat16).at[slot_index]  23.1 us
    dot_general x1, matrix products, per_device(): jnp.dot(hidden, down_full, preferred_element_type=jnp.float32)  22.7 us
    dot_general x1, matrix products, per_device(): gate_pre = jnp.dot(rows, gate_full.T, preferred_element_type=jnp.float32)  12.8 us
    gather x1, local copies, waits for them, and re-layouts, per_device(): back_rows = returned.reshape(n_expert * CAP, model_width)[slot_index]  11.7 us
  transfers between devices with their start and end apart: 7, of which 7 were waited for; matrix products, arithmetic and copies ran while one was open for 9% of the time, Pallas kernels for 0%

commit v1 on v0

--- a/solution.py
+++ b/solution.py
@@ -12,7 +12,9 @@
     other = lax.dynamic_index_in_dim(piece, 1 - core, 0, keepdims=False)
     got = lax.ppermute(other, "core", [(0, 1), (1, 0)])
     pair = jnp.stack([mine, got])
-    return lax.all_gather(pair, "chip", axis=0, tiled=True).reshape(-1, piece.shape[-1])
+    return jnp.concatenate(
+        lax.all_to_all(jnp.stack([pair] * lax.axis_size("chip")), "chip", 0, 0), axis=0
+    ).reshape(-1, piece.shape[-1])
 
 
 def per_device(tokens, expert_ids, combine, gate_weight, up_weight, down_weight):

time: 446 us -> 492 us (1.10)
  waiting for transfers between devices: 260 us -> 358 us
  blocking collectives: 70.3 us -> 0 us
  starting transfers between devices: 8.33 us -> 32.9 us
  between operations: 13.3 us -> 0.17 us
  local copies, waits for them, and re-layouts: 45.4 us -> 53.3 us
    all_to_all x0 -> x4, waiting for transfers between devices: none -> 287 us  [the longest x3 221 us: gather_expert(): lax.all_to_all(jnp.stack([pair] * lax.axis_size('chip')), 'chip', 0, 0)]
    all_gather x3 -> x0, waiting for transfers between devices: 190 us -> none  [gather_expert(): lax.all_gather(pair, 'chip', axis=0, tiled=True)]
    all_to_all x1 -> x0, blocking collectives: 70.3 us -> none  [per_device(): arrived = lax.all_to_all(outgoing, ('expert', 'core'), 0, 0, tiled=True)]
    all_to_all x0 -> x4, starting transfers between devices: none -> 22.6 us  [the longest x3 16.4 us: gather_expert(): lax.all_to_all(jnp.stack([pair] * lax.axis_size('chip')), 'chip', 0, 0)]
    another operation x0 -> x3, local copies, waits for them, and re-layouts: none -> 9.51 us  [gather_expert(): jnp.stack([pair] * lax.axis_size('chip'))]
  transfers between devices with their start and end apart: 7 -> 8, of which waited for: 7 -> 8; matrix products, arithmetic and copies ran while one was open for 9% -> 3% of each run, Pallas kernels for 0% -> 0%
where the time goes in v1:
time: 492 us
  waiting for transfers between devices  358 us (73%)
  local copies, waits for them, and re-layouts  53.3 us (11%)
  matrix products  35.5 us (7%)
  starting transfers between devices  32.9 us (7%)
  other arithmetic  11.4 us (2%)
    all_to_all x3, waiting for transfers between devices, gather_expert(): lax.all_to_all(jnp.stack([pair] * lax.axis_size('chip')), 'chip', 0, 0)  221 us
    all_to_all x1, waiting for transfers between devices, per_device(): returned = lax.all_to_all(produced, ('expert', 'core'), 0, 0, tiled=True)  67.4 us
    all_to_all x1, waiting for transfers between devices, per_device(): arrived = lax.all_to_all(outgoing, ('expert', 'core'), 0, 0, tiled=True)  65.5 us
    scatter x1, local copies, waits for them, and re-layouts, per_device(): jnp.zeros((n_expert * CAP, model_width), jnp.bfloat16).at[slot_index]  23.1 us
    dot_general x1, matrix products, per_device(): jnp.dot(hidden, down_full, preferred_element_type=jnp.float32)  22.7 us
    all_to_all x3, starting transfers between devices, gather_expert(): lax.all_to_all(jnp.stack([pair] * lax.axis_size('chip')), 'chip', 0, 0)  16.4 us
    dot_general x1, matrix products, per_device(): gate_pre = jnp.dot(rows, gate_full.T, preferred_element_type=jnp.float32)  12.8 us
    gather x1, local copies, waits for them, and re-layouts, per_device(): back_rows = returned.reshape(n_expert * CAP, model_width)[slot_index]  11.7 us
  transfers between devices with their start and end apart: 8, of which 8 were waited for; matrix products, arithmetic and copies ran while one was open for 3% of the time, Pallas kernels for 0%

profile of v1, /device:TPU:49, one launch (start us, length us, event | category | flops | bytes accessed | tf_op | source)
XLA Modules:
  0.0 491.6 jit_solution(9438458804622632527)
XLA Ops:
  0.0 0.8 broadcast_multiply_fusion
  0.8 0.8 copy.9
  1.6 0.1 copy.8
  1.7 0.1 mul.36
  1.9 0.1 eq.22
  2.0 2.0 reduce-window.6
  4.0 0.3 slice_reduce_fusion
  4.5 23.1 %scatter_custom_fusion = bf16[1152,2048]{1,0:T(8,128)(2,1)} fusion(s32[864]{0:T(1024)S(1)} %fusion.6, bf16[144,2048]{1,0:T(8,128)(2,1)S(1)} %copy-done, s32[1024]{0:T(1024)S(1)} %pad_clamp_fusion.1, bf16[]{:T(256)} %constant.40.clone.1), kind=kCustom, calls=%fused_computation.7 | custom fusion | bytes 4718594 | tf_op jit(solution)/shard_map/scatter | solution.py:37
  27.7 6.2 %all-to-all-start = ((bf16[16,72,2048]{2,1,0:T(8,128)(2,1)}), bf16[16,72,2048]{2,1,0:T(8,128)(2,1)}, u32[]{:S(2)}, u32[]{:S(2)}) async-start(bf16[16,72,2048]{2,1,0:T(8,128)(2,1)} %bitcast.43), calls=%async_computation | async-start | bytes 9437184 | tf_op jit(solution)/shard_map/all_to_all | solution.py:40
  33.9 0.4 collective-permute-start.2
  34.3 1.4 collective-permute-done.2
  35.8 65.5 %all-to-all-done = bf16[16,72,2048]{2,1,0:T(8,128)(2,1)} async-done(((bf16[16,72,2048]{2,1,0:T(8,128)(2,1)}), bf16[16,72,2048]{2,1,0:T(8,128)(2,1)}, u32[]{:S(2)}, u32[]{:S(2)}) %all-to-all-start) | async-done | bytes 4718624 | tf_op jit(solution)/shard_map/all_to_all | solution.py:40
  101.3 3.2 stack.26
  104.5 6.6 %all-to-all-start.3 = ((bf16[8,2,88,2048]{3,2,1,0:T(8,128)(2,1)}), bf16[8,2,88,2048]{3,2,1,0:T(8,128)(2,1)}, u32[]{:S(2)}, u32[]{:S(2)}) async-start(bf16[8,2,88,2048]{3,2,1,0:T(8,128)(2,1)} %stack.26), calls=%async_computation.3 | async-start | bytes 11534336 | tf_op jit(solution)/shard_map/all_to_all | solution.py:16
  111.2 0.6 collective-permute-start
  111.7 1.3 collective-permute-done
  113.1 78.3 %all-to-all-done.3 = bf16[8,2,88,2048]{3,2,1,0:T(8,128)(2,1)} async-done(((bf16[8,2,88,2048]{3,2,1,0:T(8,128)(2,1)}), bf16[8,2,88,2048]{3,2,1,0:T(8,128)(2,1)}, u32[]{:S(2)}, u32[]{:S(2)}) %all-to-all-start.3) | async-done | bytes 5767200 | tf_op jit(solution)/shard_map/all_to_all | solution.py:16
  191.4 3.2 stack.20
  194.5 5.1 %all-to-all-start.1 = ((bf16[8,2,88,2048]{3,2,1,0:T(8,128)(2,1)}), bf16[8,2,88,2048]{3,2,1,0:T(8,128)(2,1)}, u32[]{:S(2)}, u32[]{:S(2)}) async-start(bf16[8,2,88,2048]{3,2,1,0:T(8,128)(2,1)} %stack.20), calls=%async_computation.1 | async-start | bytes 11534336 | tf_op jit(solution)/shard_map/all_to_all | solution.py:16
  199.7 1.7 collective-permute-start.1
  201.4 1.3 collective-permute-done.1
  202.8 76.5 %all-to-all-done.1 = bf16[8,2,88,2048]{3,2,1,0:T(8,128)(2,1)} async-done(((bf16[8,2,88,2048]{3,2,1,0:T(8,128)(2,1)}), bf16[8,2,88,2048]{3,2,1,0:T(8,128)(2,1)}, u32[]{:S(2)}, u32[]{:S(2)}) %all-to-all-start.1) | async-done | bytes 5767200 | tf_op jit(solution)/shard_map/all_to_all | solution.py:16
  279.4 3.2 stack.23
  282.5 4.7 all-to-all-start.2
  287.2 12.8 %fusion.8 = f32[1152,1408]{1,0:T(8,128)} fusion(bf16[1152,2048]{1,0:T(8,128)(2,1)} %bitcast.2, bf16[1408,2048]{1,0:T(8,128)(2,1)} %bitcast.5), kind=kOutput, calls=%fused_computation.40 | convolution fusion | flops 6643777536 | bytes 16973824 | tf_op jit(solution)/shard_map/dot_general | solution.py:42
  300.0 66.6 %all-to-all-done.2 = bf16[8,2,88,2048]{3,2,1,0:T(8,128)(2,1)} async-done(((bf16[8,2,88,2048]{3,2,1,0:T(8,128)(2,1)}), bf16[8,2,88,2048]{3,2,1,0:T(8,128)(2,1)}, u32[]{:S(2)}, u32[]{:S(2)}) %all-to-all-start.2) | async-done | bytes 5767200 | tf_op jit(solution)/shard_map/all_to_all | solution.py:16
  366.6 22.7 %convolution_convert_fusion = bf16[1152,2048]{1,0:T(8,128)(2,1)} fusion(bf16[1408,2048]{1,0:T(8,128)(2,1)} %bitcast.11, bf16[1152,2048]{1,0:T(8,128)(2,1)} %bitcast.2, bf16[1408,2048]{1,0:T(8,128)(2,1)} %bitcast.8, f32[1152,1408]{1,0:T(8,128)} %fusion.8), kind=kOutput, calls=%fused_computation.6 | convolution fusion | flops 13299646464 | bytes 27459584 | tf_op jit(solution)/shard_map/dot_general | solution.py:45
  389.4 7.6 %all-to-all-start.4 = ((bf16[16,72,2048]{2,1,0:T(8,128)(2,1)}), bf16[16,72,2048]{2,1,0:T(8,128)(2,1)}, u32[]{:S(2)}, u32[]{:S(2)}) async-start(bf16[16,72,2048]{2,1,0:T(8,128)(2,1)} %bitcast.44), calls=%async_computation.4 | async-start | bytes 9437184 | tf_op jit(solution)/shard_map/all_to_all | solution.py:47
  397.2 67.4 %all-to-all-done.4 = bf16[16,72,2048]{2,1,0:T(8,128)(2,1)} async-done(((bf16[16,72,2048]{2,1,0:T(8,128)(2,1)}), bf16[16,72,2048]{2,1,0:T(8,128)(2,1)}, u32[]{:S(2)}, u32[]{:S(2)}) %all-to-all-start.4) | async-done | bytes 4718624 | tf_op jit(solution)/shard_map/all_to_all | solution.py:47
  464.5 11.7 %gather_fusion = bf16[864,2048]{1,0:T(8,128)(2,1)} fusion(bf16[1152,2048]{1,0:T(8,128)(2,1)} %bitcast.13, s32[1024]{0:T(1024)S(1)} %pad_clamp_fusion), kind=kCustom, calls=%fused_computation.1 | custom fusion | bytes 7081344 | tf_op jit(solution)/shard_map/gather | solution.py:48
  476.2 7.2 %reshape.114 = f32[144,6,2048]{2,1,0:T(8,128)} reshape(bf16[864,2048]{1,0:T(8,128)(2,1)} %gather_fusion) | data formatting | bytes 10616832 | tf_op jit(solution)/shard_map/convert_element_type | solution.py:50
  483.4 8.2 %multiply_reduce_fusion = bf16[144,2048]{1,0:T(8,128)(2,1)} fusion(f32[144,6,2048]{2,1,0:T(8,128)} %reshape.114, f32[144,6]{1,0:T(8,128)S(1)} %copy.12), kind=kLoop, calls=%fused_computation.4 | loop fusion | flops 3244032 | bytes 7671168 | tf_op jit(solution)/shard_map/reduce_sum | solution.py:52
  (28 shorter events, 0.7 us)
Async XLA Ops:
  0.0 4.5 copy-start
  27.7 6.2 %copy-start.2 = (bf16[2,88,2048]{2,1,0:T(8,128)(2,1)S(1)}, bf16[2,88,2048]{2,1,0:T(8,128)(2,1)}, u32[]{:S(2)}) copy-start(bf16[2,88,2048]{2,1,0:T(8,128)(2,1)} %param.11) | copy-start | bytes 2162692
  27.7 73.7 %all-to-all-start = ((bf16[16,72,2048]{2,1,0:T(8,128)(2,1)}), bf16[16,72,2048]{2,1,0:T(8,128)(2,1)}, u32[]{:S(2)}, u32[]{:S(2)}) async-start(bf16[16,72,2048]{2,1,0:T(8,128)(2,1)} %bitcast.43), calls=%async_computation | async-start | bytes 9437184 | tf_op jit(solution)/shard_map/all_to_all | solution.py:40
  33.9 1.9 collective-permute-start.2
  104.5 6.6 %copy-start.3 = (bf16[2,88,2048]{2,1,0:T(8,128)(2,1)S(1)}, bf16[2,88,2048]{2,1,0:T(8,128)(2,1)}, u32[]{:S(2)}) copy-start(bf16[2,88,2048]{2,1,0:T(8,128)(2,1)} %param.9) | copy-start | bytes 2162692
  104.5 86.9 %all-to-all-start.3 = ((bf16[8,2,88,2048]{3,2,1,0:T(8,128)(2,1)}), bf16[8,2,88,2048]{3,2,1,0:T(8,128)(2,1)}, u32[]{:S(2)}, u32[]{:S(2)}) async-start(bf16[8,2,88,2048]{3,2,1,0:T(8,128)(2,1)} %stack.26), calls=%async_computation.3 | async-start | bytes 11534336 | tf_op jit(solution)/shard_map/all_to_all | solution.py:16
  111.2 1.9 collective-permute-start
  194.5 5.1 %copy-start.4 = (bf16[2,88,2048]{2,1,0:T(8,128)(2,1)S(1)}, bf16[2,88,2048]{2,1,0:T(8,128)(2,1)}, u32[]{:S(2)}) copy-start(bf16[2,88,2048]{2,1,0:T(8,128)(2,1)} %param.10) | copy-start | bytes 2162692
  194.5 84.8 %all-to-all-start.1 = ((bf16[8,2,88,2048]{3,2,1,0:T(8,128)(2,1)}), bf16[8,2,88,2048]{3,2,1,0:T(8,128)(2,1)}, u32[]{:S(2)}, u32[]{:S(2)}) async-start(bf16[8,2,88,2048]{3,2,1,0:T(8,128)(2,1)} %stack.20), calls=%async_computation.1 | async-start | bytes 11534336 | tf_op jit(solution)/shard_map/all_to_all | solution.py:16
  199.7 3.0 collective-permute-start.1
  282.5 84.1 %all-to-all-start.2 = ((bf16[8,2,88,2048]{3,2,1,0:T(8,128)(2,1)}), bf16[8,2,88,2048]{3,2,1,0:T(8,128)(2,1)}, u32[]{:S(2)}, u32[]{:S(2)}) async-start(bf16[8,2,88,2048]{3,2,1,0:T(8,128)(2,1)} %stack.23), calls=%async_computation.2 | async-start | bytes 11534336 | tf_op jit(solution)/shard_map/all_to_all | solution.py:16
  389.4 7.7 %copy-start.5 = (f32[144,6]{0,1:T(8,128)S(1)}, f32[144,6]{0,1:T(8,128)}, u32[]{:S(2)}) copy-start(f32[144,6]{0,1:T(8,128)} %param.8) | copy-start | bytes 10372
  389.4 75.1 %all-to-all-start.4 = ((bf16[16,72,2048]{2,1,0:T(8,128)(2,1)}), bf16[16,72,2048]{2,1,0:T(8,128)(2,1)}, u32[]{:S(2)}, u32[]{:S(2)}) async-start(bf16[16,72,2048]{2,1,0:T(8,128)(2,1)} %bitcast.44), calls=%async_computation.4 | async-start | bytes 9437184 | tf_op jit(solution)/shard_map/all_to_all | solution.py:47
  476.2 15.4 %copy-start.1 = (bf16[144,2048]{1,0:T(8,128)(2,1)S(1)}, bf16[144,2048]{1,0:T(8,128)(2,1)}, u32[]{:S(2)}) copy-start(bf16[144,2048]{1,0:T(8,128)(2,1)} %param.6) | copy-start | bytes 1769476
